TPU v7x, 32 devices: a whole 2x2x4 slice. The times are simulated.
32 devices in a mesh: heads: 4 (over y, core), seq: 8 (over z, x).
Axes of the slice: x: 2, y: 2, z: 4, core: 2. Of those that a mesh axis runs over, the one named last changes fastest.
Arguments:
- queries: bfloat16 [1024, 64, 576], P('seq', 'heads'), may hold values from -6 to 6
- latents: bfloat16 [8, 128, 576], P('seq', 'heads'), may hold values from -6 to 6
- grad_out: bfloat16 [1024, 64, 512], P('seq', 'heads'), may hold values from -6 to 6
- selected: int32 [8, 4], P('seq'), may hold values from 0 to 7, as said below
Outputs:
- output: bfloat16 [1024, 64, 512], P('seq', 'heads')
- grad_query: bfloat16 [1024, 64, 576], P('seq', 'heads')
- latent_grad: float32 [8, 128, 576], P('seq', 'heads')
Inputs may be any that keep to these rules, and one draw needn't show every extreme that they name: `selected`: row i lists 4 different blocks, none of them held on the same index of seq as block i (blocks i and j share it when i // 1 equals j // 1); how often a block is chosen varies widely between blocks.
All inputs are finite; a program needn't handle non-finite values.
Results may differ from a plain program's by a relative error of at most 0.012.
Values may be sent and summed in bfloat16 or wider, within the bound.
A program may use at most 64 MiB of HBM per device.

v0:
```python
import jax
import jax.numpy as jnp
from jax import lax
from jax.sharding import PartitionSpec as P


def shards(queries, latents, grad_out, selected):
    block_count, row_share, key_width = latents.shape
    token_total, head_count, _ = queries.shape
    value_width = grad_out.shape[2]
    key_blocks = selected.shape[1] + 1
    block_size = token_total // block_count
    score_scale = key_width ** (-0.5)
    slices = lax.all_gather(latents, "seq", axis=0, tiled=True)
    list_blocks = slices.shape[0]
    own_blocks = lax.axis_index("seq") * block_count + jnp.arange(block_count, dtype=jnp.int32)
    block_ids = jnp.concatenate([own_blocks[:, None], selected], axis=1).reshape(-1)
    picked = jnp.take(slices, block_ids, axis=0)
    key_row_tiles = lax.all_gather(picked, "heads", axis=1, tiled=True)
    key_row_tiles = key_row_tiles.reshape(block_count, key_blocks * block_size, key_width)
    value_rows = key_row_tiles[:, :, :value_width]
    query_row_tiles = queries.reshape(block_count, block_size, head_count, key_width)
    grad_rows = grad_out.reshape(block_count, block_size, head_count, value_width)
    scores = (
        jnp.einsum(
            "gonv,gmv->gnom", query_row_tiles, key_row_tiles, preferred_element_type=jnp.float32
        )
        * score_scale
    )
    prob_full = jax.nn.softmax(scores, axis=-1)
    prob_half = prob_full.astype(jnp.bfloat16)
    output = jnp.einsum(
        "bhtk,bkl->bthl", prob_half, value_rows, preferred_element_type=jnp.float32
    ).astype(jnp.bfloat16)
    row_delta = jnp.sum(grad_rows.astype(jnp.float32) * output.astype(jnp.float32), axis=-1)
    grad_prob = jnp.einsum(
        "bthl,bkl->bhtk", grad_rows, value_rows, preferred_element_type=jnp.float32
    )
    score_gradient = (
        prob_full * (grad_prob - jnp.transpose(row_delta, (0, 2, 1))[..., None]) * score_scale
    ).astype(jnp.bfloat16)
    grad_query = jnp.einsum(
        "mfgv,mvq->mgfq", score_gradient, key_row_tiles, preferred_element_type=jnp.float32
    ).astype(jnp.bfloat16)
    key_gradient = jnp.einsum(
        "jxnq,jnxa->jqa", score_gradient, query_row_tiles, preferred_element_type=jnp.float32
    )
    grad_value = jnp.einsum(
        "bhtk,bthl->bkl", prob_half, grad_rows, preferred_element_type=jnp.float32
    )
    key_gradient = jnp.concatenate(
        [key_gradient[:, :, :value_width] + grad_value, key_gradient[:, :, value_width:]], axis=-1
    )
    contrib = key_gradient.reshape(block_count * key_blocks, block_size, key_width)
    head_total = lax.psum(contrib, "heads")
    own_share = lax.dynamic_slice_in_dim(
        head_total, lax.axis_index("heads") * row_share, row_share, 1
    )
    one_hot = (jnp.arange(list_blocks, dtype=jnp.int32)[:, None] == block_ids[None, :]).astype(
        jnp.float32
    )
    dense_grad = jnp.dot(
        one_hot,
        own_share.reshape(block_count * key_blocks, row_share * key_width),
        precision=lax.Precision.HIGHEST,
        preferred_element_type=jnp.float32,
    )
    dense_grad = dense_grad.reshape(list_blocks, row_share, key_width)
    holders = list_blocks // block_count
    bundles = dense_grad.reshape(1, holders * block_count, row_share, key_width)
    arrived = lax.all_to_all(bundles, "seq", split_axis=1, concat_axis=0, tiled=True)
    latent_grad = jnp.sum(arrived, axis=0)
    return (
        output.reshape(token_total, head_count, value_width),
        grad_query.reshape(token_total, head_count, key_width),
        latent_grad,
    )


def solution(mesh):
    in_specs = (
        P("seq", "heads", None),
        P("seq", "heads", None),
        P("seq", "heads", None),
        P("seq", None),
    )
    out_specs = (P("seq", "heads", None), P("seq", "heads", None), P("seq", "heads", None))
    return jax.shard_map(shards, mesh=mesh, in_specs=in_specs, out_specs=out_specs, check_vma=False)
```

profile of v0, /device:TPU:0, one launch (start us, length us, event | category | flops | bytes accessed | tf_op | source)
XLA Modules:
  0.0 150.2 jit_solution(12962128840217296627)
XLA Ops:
  7.2 0.0 copy-start
  7.2 0.0 all-reduce.2.cloned.1.call-start
  7.2 0.9 compare_and_fusion
  8.1 32.9 %all_gather.6 = bf16[8,32,576]{2,1,0:T(8,128)(2,1)S(1)} all-gather(bf16[1,32,576]{2,1,0:T(8,128)(2,1)} %param.5), channel_id=1, replica_groups=mesh['heads'=4,'seq'=8] {'seq'}, dimensions={0}, use_global_device_ids=true | all-gather | bytes 331776 | tf_op jit(solution)/shard_map/all_gather | solution.py:14
  41.0 0.6 gather_fusion
  41.6 0.1 broadcast_select_fusion
  41.7 8.8 %all_gather.7 = bf16[5,128,576]{2,1,0:T(8,128)(2,1)S(1)} all-gather(bf16[5,32,576]{2,1,0:T(8,128)(2,1)S(1)} %broadcast_select_fusion), channel_id=1, replica_groups=mesh['heads'=4,'seq'=8] {'heads'}, dimensions={1}, use_global_device_ids=true | all-gather | bytes 921600 | tf_op jit(solution)/shard_map/all_gather | solution.py:19
  50.5 0.0 copy-start.2
  50.5 4.8 %copy.37 = bf16[128,16,512]{0,2,1:T(8,128)(2,1)} copy(bf16[128,16,512]{2,1,0:T(8,128)(2,1)} %param.6) | data formatting | bytes 4194304 | tf_op args[2]
  55.3 0.0 copy-done
  55.3 2.2 %bitcast_reduce_fusion = (f32[16,128]{1,0:T(8,128)S(1)}, f32[640,128,16]{1,0,2:T(8,128)S(1)}) fusion(bf16[640,576,1]{1,0,2:T(8,128)(2,1)S(1)} %bitcast.124, bf16[128,16,576]{0,2,1:T(8,128)(2,1)S(1)} %copy-done), kind=kOutput, calls=%fused_computation.6 | convolution fusion | flops 1512568832 | bytes 8347648 | tf_op jit(solution)/shard_map/gonv,gmv->gnom/dot_general | solution.py:25
  57.5 0.0 copy-start.1
  57.5 0.9 fusion.5
  58.4 0.7 copy-done.1
  59.1 3.5 %fusion.6 = (f32[128,16]{0,1:T(8,128)S(1)}, bf16[512,16,128]{2,0,1:T(8,128)(2,1)}) fusion(bf16[128,16,512]{0,2,1:T(8,128)(2,1)S(1)} %copy-done.1, f32[16,128]{1,0:T(8,128)S(1)} %fusion.5, f32[16,128]{1,0:T(8,128)S(1)} %get-tuple-element.14, f32[640,128,16]{1,0,2:T(8,128)S(1)} %get-tuple-element.15, bf16[1,640,576]{2,1,0:T(8,128)(2,1)S(1)} %bitcast.125), kind=kOutput, calls=%fused_computation.11 | convolution fusion | flops 1352660992 | bytes 10117120 | tf_op jit(solution)/shard_map/bhtk,bkl->bthl/dot_general | solution.py:32
  62.6 0.0 copy-done.2
  62.6 2.0 %fusion.7 = bf16[16,128,640]{1,2,0:T(8,128)(2,1)S(1)} fusion(f32[16,128]{1,0:T(8,128)S(1)} %bitcast.130, f32[16,128]{1,0:T(8,128)S(1)} %fusion.5, f32[16,128]{1,0:T(8,128)S(1)} %get-tuple-element.14, f32[640,128,16]{1,0,2:T(8,128)S(1)} %get-tuple-element.15, bf16[128,16,512]{0,2,1:T(8,128)(2,1)S(1)} %copy-done.1, bf16[1,640,576]{2,1,0:T(8,128)(2,1)S(1)} %bitcast.126), kind=kOutput, calls=%fused_computation.12 | convolution fusion | flops 1351352320 | bytes 10641408 | tf_op jit(solution)/shard_map/bthl,bkl->bhtk/dot_general | solution.py:36
  64.6 0.0 copy-start.3
  64.6 2.0 %convolution_bitcast_fusion = f32[1,640,576]{1,2,0:T(8,128)S(1)} fusion(bf16[16,128,640]{1,2,0:T(8,128)(2,1)S(1)} %fusion.7, bf16[128,16,576]{0,2,1:T(8,128)(2,1)S(1)} %copy-done), kind=kOutput, calls=%fused_computation.21 | convolution fusion | flops 1509949440 | bytes 6455296 | tf_op jit(solution)/shard_map/jxnq,jnxa->jqa/dot_general | solution.py:45
  66.6 0.0 copy-done.3
  66.6 1.9 %fusion.19 = f32[1,640,512]{1,2,0:T(8,128)S(1)} fusion(bf16[128,16,512]{0,2,1:T(8,128)(2,1)S(1)} %copy-done.1, f32[1,640,576]{1,2,0:T(8,128)S(1)} %convolution_bitcast_fusion, f32[16,128]{1,0:T(8,128)S(1)} %fusion.5, f32[16,128]{1,0:T(8,128)S(1)} %get-tuple-element.14, f32[640,128,16]{1,0,2:T(8,128)S(1)} %get-tuple-element.15), kind=kOutput, calls=%fused_computation.23 | convolution fusion | flops 1347747840 | bytes 9977856 | tf_op jit(solution)/shard_map/bhtk,bthl->bkl/dot_general | solution.py:48
  68.6 1.2 pad_maximum_fusion
  69.8 3.0 %copy.43 = f32[1,640,576]{2,1,0:T(8,128)} copy(f32[1,640,576]{1,2,0:T(8,128)} %pad_maximum_fusion) | data formatting | bytes 2949120 | tf_op jit(solution)/shard_map/concatenate | solution.py:51
  72.8 0.0 all-reduce.2.cloned.1.call-update
  72.8 44.1 %all-reduce.2.cloned.1.call-done = f32[5,128,576]{2,1,0:T(8,128)} async-done(((f32[5,128,576]{2,1,0:T(8,128)}), f32[5,128,576]{2,1,0:T(8,128)}) %all-reduce.2.cloned.1.call-update) | async-done | bytes 1474576 | tf_op jit(solution)/shard_map/psum | solution.py:55
  117.0 1.0 constant_dynamic-slice_fusion
  118.0 0.2 reshape.186
  118.2 0.2 dot_general.43
  118.4 0.7 convolution_bitcast_fusion.1
  119.1 1.0 copy.45
  120.0 5.5 %all-to-all-start = ((f32[1,8,32,576]{3,2,0,1:T(8,128)}), f32[1,8,32,576]{3,2,0,1:T(8,128)S(1)}, u32[]{:S(2)}, u32[]{:S(2)}) async-start(f32[1,8,32,576]{3,2,0,1:T(8,128)} %copy.45), calls=%async_computation | async-start | bytes 1310720 | tf_op jit(solution)/shard_map/all_to_all | solution.py:71
  125.5 4.5 %copy.46 = bf16[128,16,512]{2,1,0:T(8,128)(2,1)} copy(bf16[128,16,512]{0,2,1:T(8,128)(2,1)} %bitcast.123) | data formatting | bytes 4194304
  130.1 5.4 %convert_bitcast_fusion = bf16[128,16,576]{0,2,1:T(8,128)(2,1)} fusion(bf16[640,576,1]{1,0,2:T(8,128)(2,1)} %bitcast.127, bf16[16,128,640]{1,2,0:T(8,128)(2,1)} %copy-done.3), kind=kOutput, calls=%fused_computation.18 | convolution fusion | flops 1511129088 | bytes 5718016 | tf_op jit(solution)/shard_map/mfgv,mvq->mgfq/dot_general | solution.py:42
  135.5 7.2 %all-to-all-done = f32[1,8,32,576]{3,2,0,1:T(8,128)S(1)} async-done(((f32[1,8,32,576]{3,2,0,1:T(8,128)}), f32[1,8,32,576]{3,2,0,1:T(8,128)S(1)}, u32[]{:S(2)}, u32[]{:S(2)}) %all-to-all-start) | async-done | bytes 589856 | tf_op jit(solution)/shard_map/all_to_all | solution.py:71
  142.7 0.7 reduce_sum.34
  (3 shorter events, 0.0 us)
Async XLA Ops:
  7.2 48.1 %copy-start = (bf16[128,16,576]{0,2,1:T(8,128)(2,1)S(1)}, bf16[128,16,576]{0,2,1:T(8,128)(2,1)}, u32[]{:S(2)}) copy-start(bf16[128,16,576]{0,2,1:T(8,128)(2,1)} %param.4) | copy-start | bytes 7077892
  7.2 109.8 %all-reduce.2.cloned.1.call-start = ((), (), s32[]{:S(2)}) async-start(), calls=%async_computation.1 | async-start | bytes 3276800 | tf_op jit(solution)/shard_map/psum | solution.py:55
  50.5 12.1 %copy-start.2 = (bf16[5,128,576]{2,1,0:T(8,128)(2,1)}, bf16[5,128,576]{2,1,0:T(8,128)(2,1)S(1)}, u32[]{:S(2)}) copy-start(bf16[5,128,576]{2,1,0:T(8,128)(2,1)S(1)} %all_gather.7) | copy-start | bytes 2211844
  57.5 1.6 %copy-start.1 = (bf16[128,16,512]{0,2,1:T(8,128)(2,1)S(1)}, bf16[128,16,512]{0,2,1:T(8,128)(2,1)}, u32[]{:S(2)}) copy-start(bf16[128,16,512]{0,2,1:T(8,128)(2,1)} %copy.37) | copy-start | bytes 6291460
  64.6 2.0 %copy-start.3 = (bf16[16,128,640]{1,2,0:T(8,128)(2,1)}, bf16[16,128,640]{1,2,0:T(8,128)(2,1)S(1)}, u32[]{:S(2)}) copy-start(bf16[16,128,640]{1,2,0:T(8,128)(2,1)S(1)} %fusion.7) | copy-start | bytes 7864324
  120.0 22.7 %all-to-all-start = ((f32[1,8,32,576]{3,2,0,1:T(8,128)}), f32[1,8,32,576]{3,2,0,1:T(8,128)S(1)}, u32[]{:S(2)}, u32[]{:S(2)}) async-start(f32[1,8,32,576]{3,2,0,1:T(8,128)} %copy.45), calls=%async_computation | async-start | bytes 1310720 | tf_op jit(solution)/shard_map/all_to_all | solution.py:71
Sparse Core Ops, SparseCore 0:
  73.0 43.9 all-reduce.1
where the time goes:
time: 151 us; the launch traced here: 150 us
  waiting for transfers between devices  51.3 us (34%)
  blocking collectives  41.7 us (28%)
  matrix products  17.7 us (12%)
  local copies, waits for them, and re-layouts  16.1 us (11%)
  between operations  14.1 us (9%)
  starting transfers between devices  5.55 us (4%)
  other arithmetic  3.74 us (2%)
    psum x1, waiting for transfers between devices, shards(): head_total = lax.psum(contrib, 'heads')  44.1 us
    all_gather x1, blocking collectives, shards(): slices = lax.all_gather(latents, 'seq', axis=0, tiled=True)  32.9 us
    unnamed x10, local copies, waits for them, and re-layouts  10 us
    all_gather x1, blocking collectives, shards(): key_row_tiles = lax.all_gather(picked, 'heads', axis=1, tiled=True)  8.8 us
    all_to_all x1, waiting for transfers between devices, shards(): lax.all_to_all(bundles, 'seq', split_axis=1, concat_axis=0, tiled=True)  7.21 us
    all_to_all x1, starting transfers between devices, shards(): lax.all_to_all(bundles, 'seq', split_axis=1, concat_axis=0, tiled=True)  5.51 us
    dot_general x1, matrix products, shards(): jnp.einsum('mfgv,mvq->mgfq', score_gradient, key_row_tiles, preferred_ele...  5.43 us
    dot_general x1, matrix products, shards(): jnp.einsum('bhtk,bkl->bthl', prob_half, value_rows, preferred_element_typ...  3.47 us
  transfers between devices with their start and end apart: 2, of which 2 were waited for; matrix products, arithmetic and copies ran while one was open for 7% of the time, Pallas kernels for 0%

commit v1 on v0

--- a/solution.py
+++ b/solution.py
@@ -68,7 +68,10 @@
     dense_grad = dense_grad.reshape(list_blocks, row_share, key_width)
     holders = list_blocks // block_count
     bundles = dense_grad.reshape(1, holders * block_count, row_share, key_width)
-    arrived = lax.all_to_all(bundles, "seq", split_axis=1, concat_axis=0, tiled=True)
+    arrived = jnp.concatenate(
+        lax.all_to_all(jnp.stack(jnp.split(bundles, lax.axis_size("seq"), axis=1)), "seq", 0, 0),
+        axis=0,
+    )
     latent_grad = jnp.sum(arrived, axis=0)
     return (
         output.reshape(token_total, head_count, value_width),

time: 151 us -> 156 us (1.033)
  local copies, waits for them, and re-layouts: 16.1 us -> 20.7 us
    unnamed x10 -> x17, local copies, waits for them, and re-layouts: 10 us -> 14.9 us
  transfers between devices with their start and end apart: 2 -> 2, of which waited for: 2 -> 2; matrix products, arithmetic and copies ran while one was open for 7% -> 6% of each run, Pallas kernels for 0% -> 0%
where the time goes in v1:
time: 156 us; the launch traced here: 155 us
  waiting for transfers between devices  51.4 us (33%)
  blocking collectives  41.7 us (27%)
  local copies, waits for them, and re-layouts  20.7 us (13%)
  matrix products  17.7 us (11%)
  between operations  14.2 us (9%)
  starting transfers between devices  5.55 us (4%)
  other arithmetic  4.35 us (3%)
    psum x1, waiting for transfers between devices, shards(): head_total = lax.psum(contrib, 'heads')  44.1 us
    all_gather x1, blocking collectives, shards(): slices = lax.all_gather(latents, 'seq', axis=0, tiled=True)  32.9 us
    unnamed x17, local copies, waits for them, and re-layouts  14.9 us
    all_gather x1, blocking collectives, shards(): key_row_tiles = lax.all_gather(picked, 'heads', axis=1, tiled=True)  8.8 us
    all_to_all x1, waiting for transfers between devices, shards(): lax.all_to_all(jnp.stack(jnp.split(bundles, lax.axis_size('seq'), axis=1)...  7.21 us
    all_to_all x1, starting transfers between devices, shards(): lax.all_to_all(jnp.stack(jnp.split(bundles, lax.axis_size('seq'), axis=1)...  5.51 us
    dot_general x1, matrix products, shards(): jnp.einsum('mfgv,mvq->mgfq', score_gradient, key_row_tiles, preferred_ele...  5.43 us
    dot_general x1, matrix products, shards(): jnp.einsum('bhtk,bkl->bthl', prob_half, value_rows, preferred_element_typ...  3.47 us
  transfers between devices with their start and end apart: 2, of which 2 were waited for; matrix products, arithmetic and copies ran while one was open for 6% of the time, Pallas kernels for 0%

profile of v1, /device:TPU:0, one launch (start us, length us, event | category | flops | bytes accessed | tf_op | source)
XLA Modules:
  0.0 155.4 jit_solution(11803299763647799855)
XLA Ops:
  7.2 0.0 copy-start
  7.2 0.0 all-reduce.2.cloned.1.call-start
  7.2 0.9 compare_and_fusion
  8.1 32.9 %all_gather.6 = bf16[8,32,576]{2,1,0:T(8,128)(2,1)S(1)} all-gather(bf16[1,32,576]{2,1,0:T(8,128)(2,1)} %param.5), channel_id=1, replica_groups=mesh['heads'=4,'seq'=8] {'seq'}, dimensions={0}, use_global_device_ids=true | all-gather | bytes 331776 | tf_op jit(solution)/shard_map/all_gather | solution.py:14
  41.0 0.6 gather_fusion
  41.6 0.1 broadcast_select_fusion
  41.7 8.8 %all_gather.7 = bf16[5,128,576]{2,1,0:T(8,128)(2,1)S(1)} all-gather(bf16[5,32,576]{2,1,0:T(8,128)(2,1)S(1)} %broadcast_select_fusion), channel_id=1, replica_groups=mesh['heads'=4,'seq'=8] {'heads'}, dimensions={1}, use_global_device_ids=true | all-gather | bytes 921600 | tf_op jit(solution)/shard_map/all_gather | solution.py:19
  50.5 0.0 copy-start.2
  50.5 4.8 %copy.37 = bf16[128,16,512]{0,2,1:T(8,128)(2,1)} copy(bf16[128,16,512]{2,1,0:T(8,128)(2,1)} %param.6) | data formatting | bytes 4194304 | tf_op args[2]
  55.3 0.0 copy-done
  55.3 2.2 %bitcast_reduce_fusion = (f32[16,128]{1,0:T(8,128)S(1)}, f32[640,128,16]{1,0,2:T(8,128)S(1)}) fusion(bf16[640,576,1]{1,0,2:T(8,128)(2,1)S(1)} %bitcast.156, bf16[128,16,576]{0,2,1:T(8,128)(2,1)S(1)} %copy-done), kind=kOutput, calls=%fused_computation.6 | convolution fusion | flops 1512568832 | bytes 8347648 | tf_op jit(solution)/shard_map/gonv,gmv->gnom/dot_general | solution.py:25
  57.5 0.0 copy-start.1
  57.5 0.9 fusion.5
  58.4 0.7 copy-done.1
  59.1 3.5 %fusion.6 = (f32[128,16]{0,1:T(8,128)S(1)}, bf16[512,16,128]{2,0,1:T(8,128)(2,1)}) fusion(bf16[128,16,512]{0,2,1:T(8,128)(2,1)S(1)} %copy-done.1, f32[16,128]{1,0:T(8,128)S(1)} %fusion.5, f32[16,128]{1,0:T(8,128)S(1)} %get-tuple-element.14, f32[640,128,16]{1,0,2:T(8,128)S(1)} %get-tuple-element.15, bf16[1,640,576]{2,1,0:T(8,128)(2,1)S(1)} %bitcast.157), kind=kOutput, calls=%fused_computation.11 | convolution fusion | flops 1352660992 | bytes 10117120 | tf_op jit(solution)/shard_map/bhtk,bkl->bthl/dot_general | solution.py:32
  62.6 0.0 copy-done.2
  62.6 2.0 %fusion.7 = bf16[16,128,640]{1,2,0:T(8,128)(2,1)S(1)} fusion(f32[16,128]{1,0:T(8,128)S(1)} %bitcast.162, f32[16,128]{1,0:T(8,128)S(1)} %fusion.5, f32[16,128]{1,0:T(8,128)S(1)} %get-tuple-element.14, f32[640,128,16]{1,0,2:T(8,128)S(1)} %get-tuple-element.15, bf16[128,16,512]{0,2,1:T(8,128)(2,1)S(1)} %copy-done.1, bf16[1,640,576]{2,1,0:T(8,128)(2,1)S(1)} %bitcast.158), kind=kOutput, calls=%fused_computation.12 | convolution fusion | flops 1351352320 | bytes 10641408 | tf_op jit(solution)/shard_map/bthl,bkl->bhtk/dot_general | solution.py:36
  64.6 0.0 copy-start.3
  64.6 2.0 %convolution_bitcast_fusion = f32[1,640,576]{1,2,0:T(8,128)S(1)} fusion(bf16[16,128,640]{1,2,0:T(8,128)(2,1)S(1)} %fusion.7, bf16[128,16,576]{0,2,1:T(8,128)(2,1)S(1)} %copy-done), kind=kOutput, calls=%fused_computation.21 | convolution fusion | flops 1509949440 | bytes 6455296 | tf_op jit(solution)/shard_map/jxnq,jnxa->jqa/dot_general | solution.py:45
  66.6 0.0 copy-done.3
  66.6 1.9 %fusion.19 = f32[1,640,512]{1,2,0:T(8,128)S(1)} fusion(bf16[128,16,512]{0,2,1:T(8,128)(2,1)S(1)} %copy-done.1, f32[1,640,576]{1,2,0:T(8,128)S(1)} %convolution_bitcast_fusion, f32[16,128]{1,0:T(8,128)S(1)} %fusion.5, f32[16,128]{1,0:T(8,128)S(1)} %get-tuple-element.14, f32[640,128,16]{1,0,2:T(8,128)S(1)} %get-tuple-element.15), kind=kOutput, calls=%fused_computation.23 | convolution fusion | flops 1347747840 | bytes 9977856 | tf_op jit(solution)/shard_map/bhtk,bthl->bkl/dot_general | solution.py:48
  68.5 1.2 pad_maximum_fusion
  69.8 3.0 %copy.43 = f32[1,640,576]{2,1,0:T(8,128)} copy(f32[1,640,576]{1,2,0:T(8,128)} %pad_maximum_fusion) | data formatting | bytes 2949120 | tf_op jit(solution)/shard_map/concatenate | solution.py:51
  72.8 0.0 all-reduce.2.cloned.1.call-update
  72.8 44.1 %all-reduce.2.cloned.1.call-done = f32[5,128,576]{2,1,0:T(8,128)} async-done(((f32[5,128,576]{2,1,0:T(8,128)}), f32[5,128,576]{2,1,0:T(8,128)}) %all-reduce.2.cloned.1.call-update) | async-done | bytes 1474576 | tf_op jit(solution)/shard_map/psum | solution.py:55
  117.0 1.0 constant_dynamic-slice_fusion
  118.0 0.2 reshape.185
  118.2 0.2 dot_general.43
  118.4 0.7 convolution_bitcast_fusion.1
  119.1 0.7 fusion.30
  119.7 0.7 fusion.29
  120.4 0.7 fusion.28
  121.1 0.7 fusion.27
  121.8 0.7 fusion.26
  122.5 0.7 fusion.25
  123.2 0.7 fusion.24
  123.9 0.7 fusion.23
  124.6 5.5 %all-to-all-start = ((f32[8,1,1,32,576]{4,1,3,2,0:T(1,128)}), f32[8,1,1,32,576]{4,1,3,2,0:T(1,128)S(1)}, u32[]{:S(2)}, u32[]{:S(2)}) async-start(f32[8,1,1,32,576]{4,1,3,2,0:T(1,128)} %fusion.23), calls=%async_computation | async-start | bytes 1310720 | tf_op jit(solution)/shard_map/all_to_all | solution.py:72
  130.2 4.5 %copy.45 = bf16[128,16,512]{2,1,0:T(8,128)(2,1)} copy(bf16[128,16,512]{0,2,1:T(8,128)(2,1)} %bitcast.155) | data formatting | bytes 4194304
  134.7 5.4 %convert_bitcast_fusion = bf16[128,16,576]{0,2,1:T(8,128)(2,1)} fusion(bf16[640,576,1]{1,0,2:T(8,128)(2,1)} %bitcast.159, bf16[16,128,640]{1,2,0:T(8,128)(2,1)} %copy-done.3), kind=kOutput, calls=%fused_computation.18 | convolution fusion | flops 1511129088 | bytes 5718016 | tf_op jit(solution)/shard_map/mfgv,mvq->mgfq/dot_general | solution.py:42
  140.1 7.2 %all-to-all-done = f32[8,1,1,32,576]{4,1,3,2,0:T(1,128)S(1)} async-done(((f32[8,1,1,32,576]{4,1,3,2,0:T(1,128)}), f32[8,1,1,32,576]{4,1,3,2,0:T(1,128)S(1)}, u32[]{:S(2)}, u32[]{:S(2)}) %all-to-all-start) | async-done | bytes 589856 | tf_op jit(solution)/shard_map/all_to_all | solution.py:72
  147.3 1.3 reduce_sum.34
  (3 shorter events, 0.0 us)
Async XLA Ops:
  7.2 48.1 %copy-start = (bf16[128,16,576]{0,2,1:T(8,128)(2,1)S(1)}, bf16[128,16,576]{0,2,1:T(8,128)(2,1)}, u32[]{:S(2)}) copy-start(bf16[128,16,576]{0,2,1:T(8,128)(2,1)} %param.4) | copy-start | bytes 7077892
  7.2 109.8 %all-reduce.2.cloned.1.call-start = ((), (), s32[]{:S(2)}) async-start(), calls=%async_computation.1 | async-start | bytes 3276800 | tf_op jit(solution)/shard_map/psum | solution.py:55
  50.5 12.1 %copy-start.2 = (bf16[5,128,576]{2,1,0:T(8,128)(2,1)}, bf16[5,128,576]{2,1,0:T(8,128)(2,1)S(1)}, u32[]{:S(2)}) copy-start(bf16[5,128,576]{2,1,0:T(8,128)(2,1)S(1)} %all_gather.7) | copy-start | bytes 2211844
  57.5 1.6 %copy-start.1 = (bf16[128,16,512]{0,2,1:T(8,128)(2,1)S(1)}, bf16[128,16,512]{0,2,1:T(8,128)(2,1)}, u32[]{:S(2)}) copy-start(bf16[128,16,512]{0,2,1:T(8,128)(2,1)} %copy.37) | copy-start | bytes 6291460
  64.6 2.0 %copy-start.3 = (bf16[16,128,640]{1,2,0:T(8,128)(2,1)}, bf16[16,128,640]{1,2,0:T(8,128)(2,1)S(1)}, u32[]{:S(2)}) copy-start(bf16[16,128,640]{1,2,0:T(8,128)(2,1)S(1)} %fusion.7) | copy-start | bytes 7864324
  124.6 22.7 %all-to-all-start = ((f32[8,1,1,32,576]{4,1,3,2,0:T(1,128)}), f32[8,1,1,32,576]{4,1,3,2,0:T(1,128)S(1)}, u32[]{:S(2)}, u32[]{:S(2)}) async-start(f32[8,1,1,32,576]{4,1,3,2,0:T(1,128)} %fusion.23), calls=%async_computation | async-start | bytes 1310720 | tf_op jit(solution)/shard_map/all_to_all | solution.py:72
Sparse Core Ops, SparseCore 0:
  72.9 43.9 all-reduce.1
